TPU v7x, 32 devices: a whole 2x2x4 slice. The times are simulated.
32 devices in a mesh: ep: 16 (over z, x, core), hs: 2 (over y).
Axes of the slice: x: 2, y: 2, z: 4, core: 2. Of those that a mesh axis runs over, the one named last changes fastest.
Arguments:
- tokens: bfloat16 [8192, 1024], P(('ep', 'hs')), may hold values from -6 to 6
- segment_ids: int32 [32, 256], P(('ep', 'hs')), may hold values from 0 to 3, never falling along the last dimension, each value on 1 to 128 neighbouring positions
- live_mask: int32 [32, 256], P(('ep', 'hs')), may hold values 0 or 1
- routes: int32 [8192, 8], P(('ep', 'hs')), may hold values from 0 to 15, all different within a row; in each aligned block of 256 rows (0 to 255, 256 to 511, ...) at most 256 rows name the same one
- attn_gain: float32 [1024], replicated, may hold values from 0.25 to 1.75
- w_query: bfloat16 [1024, 1024], replicated, may hold values from -0.1875 to 0.1875
- key_weight: bfloat16 [1024, 512], replicated, may hold values from -0.1875 to 0.1875
- value_weight: bfloat16 [1024, 512], replicated, may hold values from -0.1875 to 0.1875
- w_out: bfloat16 [1024, 1024], replicated, may hold values from -1 to 1
- moe_gain: float32 [1024], replicated, may hold values from 0.25 to 1.75
- router: bfloat16 [1024, 16], replicated, may hold values from -0.09375 to 0.09375
- w_gate: bfloat16 [16, 1024, 512], P('ep', None, 'hs'), may hold values from -0.1875 to 0.1875
- w_up: bfloat16 [16, 1024, 512], P('ep', None, 'hs'), may hold values from -0.1875 to 0.1875
- w_down: bfloat16 [16, 512, 1024], P('ep', 'hs'), may hold values from -0.75 to 0.75
- cotangent: bfloat16 [8192, 1024], P(('ep', 'hs')), may hold values from -6 to 6
Outputs:
- output: bfloat16 [8192, 1024], P(('ep', 'hs'))
- input_grad: float32 [8192, 1024], P(('ep', 'hs'))
- attn_gain_grad: float32 [1024], replicated
- query_grad: float32 [1024, 1024], replicated
- key_grad: float32 [1024, 512], replicated
- value_grad: float32 [1024, 512], replicated
- out_grad: float32 [1024, 1024], replicated
- moe_gain_grad: float32 [1024], replicated
- router_grad: float32 [1024, 16], replicated
- gate_grad: float32 [16, 1024, 512], P('ep', None, 'hs')
- up_grad: float32 [16, 1024, 512], P('ep', None, 'hs')
- down_grad: float32 [16, 512, 1024], P('ep', 'hs')
- expert_counts: int32 [16], replicated
Inputs may be any that keep to these rules, and one draw needn't show every extreme that they name: `segment_ids`: document numbers never fall along a row; a document has at most 128 tokens, and one has exactly that many. `routes`: each token names 8 different experts. The 256 tokens of one row name one expert at most 256 times, a bound that some block reaches.
All inputs are finite; a program needn't handle non-finite values. No bound on the sum of `live_mask` on one device may be relied on, other than what follows from the above.
Results may differ from a plain program's by a relative error of at most 0.013.
The roundings to bfloat16 on the way count: a program that leaves them out, or rounds other values in their place, can miss the bound.
Values may be sent and summed in bfloat16 or wider, within the bound.
A program may use at most 384 MiB of HBM per device.

v0:
```python
import jax
import jax.numpy as jnp
from jax import lax
from jax.sharding import PartitionSpec as P

QUERY_HEADS = 16
KEY_VALUE_HEADS = 8
HEAD_SIZE = 64
TOP = 8
EPSILON = 1e-05


def rms_forward(value_rows, norm_gain):
    inverse = lax.rsqrt(jnp.mean(value_rows * value_rows, axis=-1, keepdims=True) + EPSILON)
    return (value_rows * inverse * norm_gain, inverse)


def rms_backward(value_rows, inverse, norm_gain, upstream):
    scaled = upstream * norm_gain
    gain_grad = jnp.sum(upstream * value_rows * inverse, axis=0)
    input_grad = inverse * (
        scaled
        - value_rows * inverse * inverse * jnp.mean(scaled * value_rows, axis=-1, keepdims=True)
    )
    return (input_grad, gain_grad)


def positions_of(segment):
    sequence_length = segment.shape[-1]
    indices = jnp.arange(sequence_length, dtype=jnp.int32)
    starts = jnp.concatenate([jnp.ones((1,), dtype=bool), segment[1:] != segment[:-1]])
    first_index = lax.cummax(jnp.where(starts, indices, 0), axis=0)
    return indices - first_index


def rotary_tables(positions, head_dim):
    half_dim = head_dim // 2
    frequency = 10000.0 ** (-(jnp.arange(half_dim, dtype=jnp.float32) * 2.0) / head_dim)
    angles = positions.astype(jnp.float32)[:, None] * frequency[None, :]
    return (jnp.cos(angles)[:, None, :], jnp.sin(angles)[:, None, :])


def rotary(heads, cosine_table, sine_table):
    half_dim = heads.shape[-1] // 2
    first_half = heads[..., :half_dim]
    second_half = heads[..., half_dim:]
    return jnp.concatenate(
        [
            first_half * cosine_table - second_half * sine_table,
            second_half * cosine_table + first_half * sine_table,
        ],
        axis=-1,
    )


def rotary_backward(grads, cosine_table, sine_table):
    half_dim = grads.shape[-1] // 2
    first_half = grads[..., :half_dim]
    second_half = grads[..., half_dim:]
    return jnp.concatenate(
        [
            first_half * cosine_table + second_half * sine_table,
            second_half * cosine_table - first_half * sine_table,
        ],
        axis=-1,
    )


def rounded(value_rows):
    return lax.optimization_barrier(value_rows.astype(jnp.bfloat16)).astype(jnp.float32)


def hidden_units(slot_rows, gate_w, up_w):
    gate_pre = jnp.einsum("red,edf->ref", slot_rows, gate_w, preferred_element_type=jnp.float32)
    up_pre = jnp.einsum("red,edf->ref", slot_rows, up_w, preferred_element_type=jnp.float32)
    return (gate_pre, up_pre)


def expert_rows(slot_rows, gate_w, up_w, down_w):
    gate_pre, up_pre = hidden_units(slot_rows, gate_w, up_w)
    hidden = (jax.nn.silu(gate_pre) * up_pre).astype(jnp.bfloat16)
    partial_value = jnp.einsum("ref,efd->red", hidden, down_w, preferred_element_type=jnp.float32)
    total = rounded(partial_value)
    return total


def hidden_grads(slot_rows, upstream, gate_w, up_w, down_w):
    gate_pre, up_pre = hidden_units(slot_rows, gate_w, up_w)
    sigmoid_part = jax.nn.sigmoid(gate_pre)
    activated = gate_pre * sigmoid_part
    hidden = (activated * up_pre).astype(jnp.bfloat16)
    hidden_grad = jnp.einsum("red,efd->ref", upstream, down_w, preferred_element_type=jnp.float32)
    up_pre_grad = (hidden_grad * activated).astype(jnp.bfloat16)
    gate_pre_grad = (
        hidden_grad * up_pre * sigmoid_part * (1.0 + gate_pre * (1.0 - sigmoid_part))
    ).astype(jnp.bfloat16)
    down_w_grad = jnp.einsum("ref,red->efd", hidden, upstream, preferred_element_type=jnp.float32)
    gate_w_grad = jnp.einsum(
        "red,ref->edf", slot_rows, gate_pre_grad, preferred_element_type=jnp.float32
    )
    up_w_grad = jnp.einsum(
        "red,ref->edf", slot_rows, up_pre_grad, preferred_element_type=jnp.float32
    )
    return (gate_pre_grad, up_pre_grad, gate_w_grad, up_w_grad, down_w_grad)


def input_partial(gate_pre_grad, up_pre_grad, gate_w, up_w):
    partial_value = jnp.einsum(
        "ref,edf->red", gate_pre_grad, gate_w, preferred_element_type=jnp.float32
    )
    partial_value = partial_value + jnp.einsum(
        "ref,edf->red", up_pre_grad, up_w, preferred_element_type=jnp.float32
    )
    total = rounded(partial_value)
    return total


def local(
    tokens,
    segment_ids,
    live_mask,
    routes,
    attn_gain,
    w_query,
    key_weight,
    value_weight,
    w_out,
    moe_gain,
    router,
    w_gate,
    w_up,
    w_down,
    cotangent,
):
    sequence_length = tokens.shape[0]
    model_dim = tokens.shape[1]
    experts_all = router.shape[1]
    capacity = min(sequence_length, 2 * sequence_length * TOP // experts_all)
    slots_total = capacity * experts_all
    query_per_key_head = QUERY_HEADS // KEY_VALUE_HEADS
    score_scale = HEAD_SIZE ** (-0.5)
    segment = segment_ids[0]
    live_row = live_mask[0]
    inputs = tokens.astype(jnp.float32)
    normed_rows, inverse_one = rms_forward(inputs, attn_gain)
    normed_rows_back = normed_rows.astype(jnp.bfloat16)
    query_pre = jnp.dot(normed_rows_back, w_query, preferred_element_type=jnp.float32).reshape(
        sequence_length, QUERY_HEADS, HEAD_SIZE
    )
    key_before_rotary = jnp.dot(
        normed_rows_back, key_weight, preferred_element_type=jnp.float32
    ).reshape(sequence_length, KEY_VALUE_HEADS, HEAD_SIZE)
    value_b = (
        jnp.dot(normed_rows_back, value_weight, preferred_element_type=jnp.float32)
        .astype(jnp.bfloat16)
        .reshape(sequence_length, KEY_VALUE_HEADS, HEAD_SIZE)
    )
    positions = positions_of(segment)
    cosine_table, sine_table = rotary_tables(positions, HEAD_SIZE)
    query_back_rows = rotary(query_pre, cosine_table, sine_table).astype(jnp.bfloat16)
    key_b = rotary(key_before_rotary, cosine_table, sine_table).astype(jnp.bfloat16)
    indices = jnp.arange(sequence_length)
    allowed = (
        (segment[:, None] == segment[None, :])
        & (indices[None, :] <= indices[:, None])
        & ((live_row[None, :] > 0) | (indices[None, :] == indices[:, None]))
    )
    grouped_rows = query_back_rows.reshape(
        sequence_length, KEY_VALUE_HEADS, query_per_key_head, HEAD_SIZE
    )
    scores = (
        jnp.einsum("qgrd,kgd->grqk", grouped_rows, key_b, preferred_element_type=jnp.float32)
        * score_scale
    )
    scores = jnp.where(allowed, scores, -1e30)
    highest = jnp.max(scores, axis=-1, keepdims=True)
    weights_exp = jnp.exp(scores - highest)
    denominator = jnp.sum(weights_exp, axis=-1, keepdims=True)
    log_total = highest + jnp.log(denominator)
    probabilities = weights_exp / denominator
    mixed = jnp.einsum(
        "grqk,kgd->qgrd",
        probabilities.astype(jnp.bfloat16),
        value_b,
        preferred_element_type=jnp.float32,
    )
    mixed_b = mixed.reshape(sequence_length, QUERY_HEADS * HEAD_SIZE).astype(jnp.bfloat16)
    middle = inputs + jnp.dot(mixed_b, w_out, preferred_element_type=jnp.float32)
    moe_normed, inverse_two = rms_forward(middle, moe_gain)
    moe_in = moe_normed.astype(jnp.bfloat16)
    logits = jnp.dot(moe_in, router, preferred_element_type=jnp.float32)
    route_hot = (routes[:, :, None] == jnp.arange(experts_all)[None, None, :]).astype(jnp.float32)
    chosen = jnp.sum(route_hot * logits[:, None, :], axis=-1)
    route_soft = jax.nn.softmax(chosen, axis=-1)
    live_column = live_row.astype(jnp.float32)[:, None]
    route_gates = route_soft * live_column
    counts_local = jnp.sum(route_hot * live_column[:, :, None], axis=(0, 1))
    flat_expert = routes.reshape(-1)
    assign_hot = (flat_expert[:, None] == jnp.arange(experts_all)[None, :]).astype(jnp.int32)
    running = jnp.cumsum(assign_hot, axis=0)
    slot_index = jnp.sum(assign_hot * running, axis=1) - 1
    destination = slot_index * experts_all + flat_expert
    source = (
        jnp.zeros((slots_total,), jnp.int32)
        .at[destination]
        .set(jnp.arange(sequence_length * TOP, dtype=jnp.int32))
    )
    filled = jnp.zeros((slots_total,), jnp.int32).at[destination].set(1) > 0
    token_of_slot = source // TOP
    dispatched = jnp.where(filled[:, None], moe_in[token_of_slot], jnp.zeros((), jnp.bfloat16))
    dispatched = dispatched.reshape(capacity, experts_all, model_dim)
    received = lax.all_to_all(dispatched, "ep", split_axis=1, concat_axis=0, tiled=True)
    gathered = lax.all_gather(received, "hs", axis=0, tiled=True)
    expert_sum = lax.psum_scatter(
        expert_rows(gathered, w_gate, w_up, w_down).astype(jnp.bfloat16),
        "hs",
        scatter_dimension=0,
        tiled=True,
    )
    returned = lax.all_to_all(expert_sum, "ep", split_axis=0, concat_axis=1, tiled=True)
    per_route = (
        returned.reshape(slots_total, model_dim)[destination]
        .reshape(sequence_length, TOP, model_dim)
        .astype(jnp.float32)
    )
    combined = jnp.sum(route_gates[:, :, None] * per_route, axis=1)
    output = (middle + combined).astype(jnp.bfloat16)
    upstream = cotangent.astype(jnp.float32)
    gate_upstream = jnp.sum(upstream[:, None, :] * per_route, axis=-1)
    slot_gate = route_gates.reshape(-1)[source]
    slot_upstream = jnp.where(
        filled[:, None], slot_gate[:, None] * upstream[token_of_slot], 0.0
    ).astype(jnp.bfloat16)
    slot_upstream = slot_upstream.reshape(capacity, experts_all, model_dim)
    upstream_recv = lax.all_to_all(slot_upstream, "ep", split_axis=1, concat_axis=0, tiled=True)
    rows_all, grads_all = (
        lax.all_gather(received, "hs", axis=0, tiled=True),
        lax.all_gather(upstream_recv, "hs", axis=0, tiled=True),
    )
    gate_pre_grad, up_pre_grad, gate_w_grad, up_w_grad, down_w_grad = hidden_grads(
        rows_all, grads_all, w_gate, w_up, w_down
    )
    input_sum = lax.psum_scatter(
        input_partial(gate_pre_grad, up_pre_grad, w_gate, w_up).astype(jnp.bfloat16),
        "hs",
        scatter_dimension=0,
        tiled=True,
    )
    input_back = lax.all_to_all(input_sum, "ep", split_axis=0, concat_axis=1, tiled=True)
    back_routes = input_back.reshape(slots_total, model_dim)[destination].reshape(
        sequence_length, TOP, model_dim
    )
    expert_input_grad = jnp.sum(back_routes.astype(jnp.float32), axis=1)
    soft_upstream = gate_upstream * live_column
    chosen_grad = route_soft * (
        soft_upstream - jnp.sum(route_soft * soft_upstream, axis=-1, keepdims=True)
    )
    logit_grad = jnp.sum(route_hot * chosen_grad[:, :, None], axis=1).astype(jnp.bfloat16)
    router_w_grad = jnp.einsum("td,te->de", moe_in, logit_grad, preferred_element_type=jnp.float32)
    moe_in_grad = expert_input_grad + jnp.einsum(
        "te,de->td", logit_grad, router, preferred_element_type=jnp.float32
    )
    middle_norm_grad, moe_gain_grad = rms_backward(middle, inverse_two, moe_gain, moe_in_grad)
    middle_grad = upstream + middle_norm_grad
    attn_grad_b = middle_grad.astype(jnp.bfloat16)
    out_w_grad = jnp.einsum("tm,td->md", mixed_b, attn_grad_b, preferred_element_type=jnp.float32)
    attention_mixed_grad = jnp.einsum(
        "td,md->tm", attn_grad_b, w_out, preferred_element_type=jnp.float32
    ).astype(jnp.bfloat16)
    attention_mixed_grad = attention_mixed_grad.reshape(
        sequence_length, KEY_VALUE_HEADS, query_per_key_head, HEAD_SIZE
    )
    scores_again = (
        jnp.einsum("qgrd,kgd->grqk", grouped_rows, key_b, preferred_element_type=jnp.float32)
        * score_scale
    )
    scores_again = jnp.where(allowed, scores_again, -1e30)
    probs_again = jnp.exp(scores_again - log_total)
    prob_grad = jnp.einsum(
        "qgrd,kgd->grqk", attention_mixed_grad, value_b, preferred_element_type=jnp.float32
    )
    value_per_head_grad = jnp.einsum(
        "grqk,qgrd->kgd",
        probs_again.astype(jnp.bfloat16),
        attention_mixed_grad,
        preferred_element_type=jnp.float32,
    )
    value_per_head_grad = value_per_head_grad.astype(jnp.bfloat16).reshape(
        sequence_length, KEY_VALUE_HEADS * HEAD_SIZE
    )
    row_delta = jnp.sum(probs_again * prob_grad, axis=-1, keepdims=True)
    score_grad = (probs_again * (prob_grad - row_delta)).astype(jnp.bfloat16)
    query_rot_grad = (
        jnp.einsum("grqk,kgd->qgrd", score_grad, key_b, preferred_element_type=jnp.float32)
        * score_scale
    )
    rotated_key_grad = (
        jnp.einsum("grqk,qgrd->kgd", score_grad, grouped_rows, preferred_element_type=jnp.float32)
        * score_scale
    )
    query_head_grad = (
        rotary_backward(
            query_rot_grad.reshape(sequence_length, QUERY_HEADS, HEAD_SIZE),
            cosine_table,
            sine_table,
        )
        .astype(jnp.bfloat16)
        .reshape(sequence_length, QUERY_HEADS * HEAD_SIZE)
    )
    key_head_grad = (
        rotary_backward(rotated_key_grad, cosine_table, sine_table)
        .astype(jnp.bfloat16)
        .reshape(sequence_length, KEY_VALUE_HEADS * HEAD_SIZE)
    )
    query_w_grad = jnp.einsum(
        "td,te->de", normed_rows_back, query_head_grad, preferred_element_type=jnp.float32
    )
    key_w_grad = jnp.einsum(
        "td,te->de", normed_rows_back, key_head_grad, preferred_element_type=jnp.float32
    )
    value_w_grad = jnp.einsum(
        "td,te->de", normed_rows_back, value_per_head_grad, preferred_element_type=jnp.float32
    )
    normed_grad = jnp.einsum(
        "te,de->td", query_head_grad, w_query, preferred_element_type=jnp.float32
    )
    normed_grad = normed_grad + jnp.einsum(
        "te,de->td", key_head_grad, key_weight, preferred_element_type=jnp.float32
    )
    normed_grad = normed_grad + jnp.einsum(
        "te,de->td", value_per_head_grad, value_weight, preferred_element_type=jnp.float32
    )
    input_norm_grad, attn_gain_grad = rms_backward(inputs, inverse_one, attn_gain, normed_grad)
    input_grad = middle_grad + input_norm_grad
    shared = lax.psum(
        (
            attn_gain_grad,
            query_w_grad,
            key_w_grad,
            value_w_grad,
            out_w_grad,
            moe_gain_grad,
            router_w_grad,
            counts_local,
        ),
        ("ep", "hs"),
    )
    return (
        output,
        input_grad,
        shared[0],
        shared[1],
        shared[2],
        shared[3],
        shared[4],
        shared[5],
        shared[6],
        gate_w_grad,
        up_w_grad,
        down_w_grad,
        shared[7].astype(jnp.int32),
    )


def solution(mesh):
    in_specs = (
        P(("ep", "hs"), None),
        P(("ep", "hs"), None),
        P(("ep", "hs"), None),
        P(("ep", "hs"), None),
        P(),
        P(),
        P(),
        P(),
        P(),
        P(),
        P(),
        P("ep", None, "hs"),
        P("ep", None, "hs"),
        P("ep", "hs", None),
        P(("ep", "hs"), None),
    )
    out_specs = (
        P(("ep", "hs"), None),
        P(("ep", "hs"), None),
        P(),
        P(),
        P(),
        P(),
        P(),
        P(),
        P(),
        P("ep", None, "hs"),
        P("ep", None, "hs"),
        P("ep", "hs", None),
        P(),
    )
    return jax.shard_map(local, mesh=mesh, in_specs=in_specs, out_specs=out_specs, check_vma=False)
```

profile of v0, /device:TPU:0, one launch (start us, length us, event | category | flops | bytes accessed | tf_op | source)
XLA Modules:
  0.0 1641.7 jit_solution(8741621611482871611)
XLA Ops:
  12.1 4.5 reduce-window.19
  17.4 8.1 scatter_custom_fusion.1
  25.5 8.3 scatter_custom_fusion
  38.1 2.6 fusion.111
  46.6 18.3 %gather_fusion = bf16[4096,1024]{1,0:T(8,128)(2,1)} fusion(bf16[256,1024]{1,0:T(8,128)(2,1)S(1)} %multiply_convert_fusion.3, s32[4096]{0:T(1024)S(1)} %get-tuple-element.43), kind=kCustom, calls=%fused_computation | custom fusion | bytes 16793600 | tf_op jit(solution)/shard_map/gather | solution.py:210
  64.9 16.9 %copy_select_fusion = bf16[256,16,1024]{2,0,1:T(8,128)(2,1)} fusion(bf16[256,16,1024]{2,1,0:T(8,128)(2,1)} %bitcast.241, pred[256,16]{0,1:T(8,128)(4,1)S(1)} %copy.138), kind=kLoop, calls=%fused_computation.33 | loop fusion | flops 4194304 | bytes 16781312 | tf_op jit(solution)/shard_map/jit(_where)/select_n | solution.py:210
  81.8 7.5 all-to-all-start
  93.2 23.0 %gather_fusion.2 = f32[4096]{0:T(1024)S(1)} fusion(f32[2048]{0:T(1024)S(1)} %mul.462, s32[4096]{0:T(1024)S(1)} %get-tuple-element.42), kind=kCustom, calls=%fused_computation.2 | custom fusion | bytes 49152 | tf_op jit(solution)/shard_map/gather | solution.py:230
  116.4 18.6 %gather_fusion.3 = f32[4096,1024]{1,0:T(8,128)} fusion(f32[256,1024]{1,0:T(8,128)S(1)} %convert_element_type.172, s32[4096]{0:T(1024)S(1)} %get-tuple-element.43), kind=kCustom, calls=%fused_computation.3 | custom fusion | bytes 33570816 | tf_op jit(solution)/shard_map/gather | solution.py:232
  135.0 105.1 %all-to-all-done = bf16[256,16,1024]{2,0,1:T(8,128)(2,1)} async-done(((bf16[256,16,1024]{2,0,1:T(8,128)(2,1)}), bf16[256,16,1024]{2,0,1:T(8,128)(2,1)}, u32[]{:S(2)}, u32[]{:S(2)}) %all-to-all-start) | async-done | bytes 8388640 | tf_op jit(solution)/shard_map/all_to_all | solution.py:212
  240.4 15.4 fusion.14
  255.8 218.9 %all_to_all.66 = bf16[256,16,1024]{2,0,1:T(8,128)(2,1)} all-to-all(bf16[256,16,1024]{2,0,1:T(8,128)(2,1)S(1)} %fusion.14), channel_id=1, replica_groups=mesh['ep'=16,'hs'=2] {'ep'}, dimensions={1} | all-to-all | bytes 16777216 | tf_op jit(solution)/shard_map/all_to_all | solution.py:235
  475.8 15.3 fusion.18
  493.1 7.1 fusion.15
  500.2 174.6 %all-gather.5.cloned.1.call-done = bf16[8192,1,1024]{2,0,1:T(8,128)(2,1)} async-done(((bf16[4096,1,1024]{2,0,1:T(8,128)(2,1)}), bf16[8192,1,1024]{2,0,1:T(8,128)(2,1)}) %all-gather.5.cloned.1.call-update) | async-done | bytes 16777232 | tf_op jit(solution)/shard_map/all_gather | solution.py:238
  674.8 22.0 %fusion.28 = (bf16[8192,256]{1,0:T(8,128)(2,1)}, bf16[8192,1,256]{2,0,1:T(8,128)(2,1)}, bf16[8192,256]{1,0:T(8,128)(2,1)}) fusion(f32[8192,1,256]{2,0,1:T(8,128)} %fusion.15, f32[8192,1,256]{2,0,1:T(8,128)} %fusion.18, bf16[1,256,1024]{2,1,0:T(8,128)(2,1)S(1)} %copy-done.41, bf16[8192,1,1024]{2,0,1:T(8,128)(2,1)} %all-gather.5.cloned.1.call-done), kind=kOutput, calls=%fused_computation.40 | convolution fusion | flops 4326424576 | bytes 46661632 | tf_op jit(solution)/shard_map/red,efd->ref/dot_general | solution.py:92
  696.8 10.4 convert_bitcast_fusion
  707.5 18.3 %fusion.33 = f32[8192,1024]{1,0:T(8,128)} fusion(bf16[8192,1,256]{2,0,1:T(8,128)(2,1)} %get-tuple-element.30, bf16[1,1024,256]{2,1,0:T(8,128)(2,1)} %param.26), kind=kOutput, calls=%fused_computation.47 | convolution fusion | flops 4294967296 | bytes 38273024 | tf_op jit(solution)/shard_map/ref,edf->red/dot_general | solution.py:108
  725.9 19.8 %fusion = bf16[8192,1,1024]{2,0,1:T(8,128)(2,1)} fusion(f32[8192,1024]{1,0:T(8,128)} %fusion.33, bf16[8192,256]{1,0:T(8,128)(2,1)S(1)} %copy-done.11, bf16[1,1024,256]{2,1,0:T(8,128)(2,1)} %param.27), kind=kOutput, calls=%fused_computation.8 | convolution fusion | flops 4311744512 | bytes 55050240 | tf_op jit(solution)/shard_map/ref,edf->red/dot_general | solution.py:111
  745.7 150.9 %reduce-scatter.3.cloned.1.call-done = bf16[4096,1,1024]{2,0,1:T(8,128)(2,1)} async-done(((bf16[8192,1,1024]{2,0,1:T(8,128)(2,1)}), bf16[4096,1,1024]{2,0,1:T(8,128)(2,1)}) %reduce-scatter.3.cloned.1.call-update) | async-done | bytes 8388624 | tf_op jit(solution)/shard_map/reduce_scatter | solution.py:214
  897.1 12.7 reduce.13
  909.8 14.7 reshape.555
  924.5 5.9 all-to-all-start.1
  930.4 157.6 %reduce-scatter.5.cloned.1.call-done = bf16[4096,1,1024]{2,0,1:T(8,128)(2,1)} async-done(((bf16[8192,1,1024]{2,0,1:T(8,128)(2,1)}), bf16[4096,1,1024]{2,0,1:T(8,128)(2,1)}) %reduce-scatter.5.cloned.1.call-update) | async-done | bytes 8388624 | tf_op jit(solution)/shard_map/reduce_scatter | solution.py:243
  1088.0 12.7 reduce.12
  1100.7 14.5 reshape.557
  1115.2 5.8 all-to-all-start.3
  1121.1 16.7 %reshape.556 = bf16[4096,1,1024]{2,1,0:T(2,128)(2,1)} reshape(bf16[16,2,131072]{2,1,0:T(2,128)(2,1)} %all-to-all-done.1) | data formatting | bytes 16777216
  1137.9 12.1 copy.162
  1150.0 11.3 copy.141
  1161.3 15.5 gather_fusion.1
  1176.9 6.1 fusion.25
  1185.1 86.6 %all-to-all-done.3 = bf16[16,2,131072]{2,1,0:T(2,128)(2,1)} async-done(((bf16[16,2,131072]{2,1,0:T(2,128)(2,1)}), bf16[16,2,131072]{2,1,0:T(2,128)(2,1)}, u32[]{:S(2)}, u32[]{:S(2)}) %all-to-all-start.3) | async-done | bytes 8388640 | tf_op jit(solution)/shard_map/all_to_all | solution.py:249
  1271.7 16.3 reshape.558
  1288.1 12.3 copy.163
  1300.3 11.3 copy.146
  1311.7 15.6 gather_fusion.4
  1327.3 5.6 convert_reduce_fusion
  1336.8 3.1 fusion.60
  1344.6 2.7 fusion.78
  1351.5 2.8 fusion.109
  1354.3 12.9 fusion.49
  1367.2 9.3 fusion.41
  1376.8 5.5 fusion.46
  1385.6 75.0 %all-reduce = (f32[1024]{0:T(1024)}, f32[1024]{0:T(1024)}, f32[16]{0:T(128)S(1)}) all-reduce(f32[1024]{0:T(1024)S(1)} %get-tuple-element.17, f32[1024]{0:T(1024)S(1)} %get-tuple-element.15, f32[16]{0:T(128)S(1)} %get-tuple-element.19), channel_id=1, replica_groups=mesh['ep'=16,'hs'=2] {'ep','hs'}, use_global_device_ids=true, to_apply=%region_25.26 | all-reduce | flops 2064 | bytes 16512 | tf_op jit(solution)/shard_map/psum | solution.py:335
  1461.2 3.2 fusion.67
  1464.4 159.1 %all-reduce.4.cloned.1.call-done = (f32[1024,1024]{1,0:T(8,128)}, f32[1024,512]{1,0:T(8,128)}, f32[1024,512]{1,0:T(8,128)}, f32[1024,1024]{1,0:T(8,128)}, f32[1024,16]{0,1:T(8,128)}) async-done(((f32[1024,1024]{1,0:T(8,128)}, f32[1024,512]{1,0:T(8,128)}, f32[1024,512]{1,0:T(8,128)}, f32[1024,1024]{1,0:T(8,128)}, f32[1024,16]{0,1:T(8,128)}), (f32[1024,1024]{1,0:T(8,128)}, f32[1024,512]{1,0:T(8,128)}, ...) | async-done | bytes 12648464 | tf_op jit(solution)/shard_map/psum | solution.py:335
  1623.5 4.9 copy.179
  (255 shorter events, 48.7 us)
Async XLA Ops:
  7.2 37.5 %copy-start = (bf16[1024,1024]{1,0:T(8,128)(2,1)S(1)}, bf16[1024,1024]{1,0:T(8,128)(2,1)}, u32[]{:S(2)}) copy-start(bf16[1024,1024]{1,0:T(8,128)(2,1)} %param.23) | copy-start | bytes 6291460
  7.2 28.9 %copy-start.7 = (bf16[256,1024]{1,0:T(8,128)(2,1)S(1)}, bf16[256,1024]{1,0:T(8,128)(2,1)}, u32[]{:S(2)}) copy-start(bf16[256,1024]{1,0:T(8,128)(2,1)} %param.15) | copy-start | bytes 1572868
  7.2 28.9 %copy-start.48 = (f32[1024]{0:T(1024)S(1)}, f32[1024]{0:T(1024)}, u32[]{:S(2)}) copy-start(f32[1024]{0:T(1024)} %param.19) | copy-start | bytes 12292
  12.0 28.6 %copy-start.59 = (f32[256]{0:T(256)}, f32[256]{0:T(256)S(1)}, u32[]{:S(2)}) copy-start(f32[256]{0:T(256)S(1)} %add_rsqrt_fusion.1) | copy-start | bytes 3076
  17.4 16.4 copy-start.63
  36.1 7.2 copy-start.33
  45.5 19.4 %copy-start.72 = (f32[256]{0:T(256)}, f32[256]{0:T(256)S(1)}, u32[]{:S(2)}) copy-start(f32[256]{0:T(256)S(1)} %add_rsqrt_fusion) | copy-start | bytes 3076
  46.6 18.3 %copy-start.3 = (bf16[256,1024]{1,0:T(8,128)(2,1)}, bf16[256,1024]{1,0:T(8,128)(2,1)S(1)}, u32[]{:S(2)}) copy-start(bf16[256,1024]{1,0:T(8,128)(2,1)S(1)} %multiply_convert_fusion.3) | copy-start | bytes 1572868
  81.8 7.6 copy-start.74
  81.8 8.8 copy-start.50
  81.8 10.5 copy-start.52
  81.8 158.3 %all-to-all-start = ((bf16[256,16,1024]{2,0,1:T(8,128)(2,1)}), bf16[256,16,1024]{2,0,1:T(8,128)(2,1)}, u32[]{:S(2)}, u32[]{:S(2)}) async-start(bf16[256,16,1024]{2,0,1:T(8,128)(2,1)} %copy_select_fusion), calls=%async_computation | async-start | bytes 16777216 | tf_op jit(solution)/shard_map/all_to_all | solution.py:212
  89.4 385.4 %all-gather.3.cloned.1.call-start = ((), (), s32[]{:S(2)}) async-start(), calls=%async_computation.6 | async-start | bytes 25165824 | tf_op jit(solution)/shard_map/all_gather | solution.py:213
  90.6 25.8 %copy-start.1 = (f32[256,1024]{1,0:T(8,128)}, f32[256,1024]{1,0:T(8,128)S(1)}, u32[]{:S(2)}) copy-start(f32[256,1024]{1,0:T(8,128)S(1)} %convert_element_type.172) | copy-start | bytes 3145732
  93.1 23.2 %copy-start.26 = (f32[256,8]{1,0:T(8,128)}, f32[256,8]{1,0:T(8,128)S(1)}, u32[]{:S(2)}) copy-start(f32[256,8]{1,0:T(8,128)S(1)} %copy.134) | copy-start | bytes 24580
  240.1 434.7 %all-gather.5.cloned.1.call-start = ((), (), s32[]{:S(2)}) async-start(), calls=%async_computation.8 | async-start | bytes 25165824 | tf_op jit(solution)/shard_map/all_gather | solution.py:238
  474.7 16.3 copy-start.39
  474.8 421.8 %reduce-scatter.3.cloned.1.call-start = ((), (), s32[]{:S(2)}) async-start(), calls=%async_computation.7 | async-start | bytes 25165824 | tf_op jit(solution)/shard_map/reduce_scatter | solution.py:214
  475.8 17.3 %copy-start.4 = (bf16[8192,1,1024]{2,0,1:T(8,128)(2,1)S(1)}, bf16[8192,1,1024]{2,0,1:T(8,128)(2,1)}, u32[]{:S(2)}) copy-start(bf16[8192,1,1024]{2,0,1:T(8,128)(2,1)} %all-gather.3.cloned.1.call-done) | copy-start | bytes 50331652
  493.1 181.8 %copy-start.41 = (bf16[1,256,1024]{2,1,0:T(8,128)(2,1)S(1)}, bf16[1,256,1024]{2,1,0:T(8,128)(2,1)}, u32[]{:S(2)}) copy-start(bf16[1,256,1024]{2,1,0:T(8,128)(2,1)} %param.28) | copy-start | bytes 1572868
  707.3 380.7 %reduce-scatter.5.cloned.1.call-start = ((), (), s32[]{:S(2)}) async-start(), calls=%async_computation.9 | async-start | bytes 25165824 | tf_op jit(solution)/shard_map/reduce_scatter | solution.py:243
  707.5 18.4 %copy-start.11 = (bf16[8192,256]{1,0:T(8,128)(2,1)S(1)}, bf16[8192,256]{1,0:T(8,128)(2,1)}, u32[]{:S(2)}) copy-start(bf16[8192,256]{1,0:T(8,128)(2,1)} %get-tuple-element.29) | copy-start | bytes 12582916
  924.5 190.7 %all-to-all-start.1 = ((bf16[16,2,131072]{2,1,0:T(2,128)(2,1)}), bf16[16,2,131072]{2,1,0:T(2,128)(2,1)}, u32[]{:S(2)}, u32[]{:S(2)}) async-start(bf16[16,2,131072]{2,1,0:T(2,128)(2,1)} %reshape.555), calls=%async_computation.2 | async-start | bytes 16777216 | tf_op jit(solution)/shard_map/all_to_all | solution.py:220
  1115.2 5.9 copy-start.64
  1115.2 5.9 copy-start.55
  1115.2 5.9 copy-start.57
  1115.2 156.5 %all-to-all-start.3 = ((bf16[16,2,131072]{2,1,0:T(2,128)(2,1)}), bf16[16,2,131072]{2,1,0:T(2,128)(2,1)}, u32[]{:S(2)}, u32[]{:S(2)}) async-start(bf16[16,2,131072]{2,1,0:T(2,128)(2,1)} %reshape.557), calls=%async_computation.5 | async-start | bytes 16777216 | tf_op jit(solution)/shard_map/all_to_all | solution.py:249
  1121.0 502.4 %all-reduce.4.cloned.1.call-start = ((), (), s32[]{:S(2)}) async-start(), calls=%async_computation.10 | async-start | bytes 25296896 | tf_op jit(solution)/shard_map/psum | solution.py:335
  1161.3 15.5 copy-start.2
  1161.3 15.5 copy-start.27
  1176.8 6.2 copy-start.47
  1176.8 6.2 copy-start.66
  1176.8 6.2 copy-start.68
  1176.8 6.2 copy-start.70
  1176.9 6.2 copy-start.53
  1327.2 5.7 copy-start.13
  1327.3 5.7 copy-start.51
  1327.3 5.7 copy-start.62
  1327.3 6.3 copy-start.18
  1327.3 6.3 copy-start.23
  1354.3 12.9 copy-start.9
  1354.3 22.2 %slice-start = ((s8[16777216]{0:T(1024)(128)(4,1)}), s8[4194304]{0:T(1024)(128)(4,1)S(1)}, s32[]{:S(2)}) async-start(s8[16777216]{0:T(1024)(128)(4,1)} %bitcast.245), calls=%async_computation.11 | async-start | bytes 8388608
  1354.3 22.2 %slice-start.1 = ((s8[16777216]{0:T(1024)(128)(4,1)}), s8[4194304]{0:T(1024)(128)(4,1)S(1)}, s32[]{:S(2)}) async-start(s8[16777216]{0:T(1024)(128)(4,1)} %bitcast.245), calls=%async_computation.12 | async-start | bytes 8388608
  1367.2 9.3 slice-start.2
  1367.2 9.3 slice-start.3
  1367.2 9.6 copy-start.10
  1376.8 6.3 copy-start.20
  1623.5 6.3 copy-start.21
  (39 other events, 90.1 us)
Sparse Core Ops, SparseCore 0:
  240.2 230.6 all-gather.2
  474.9 199.8 all-gather.4
  707.4 189.1 reduce-scatter.2
  898.8 189.1 reduce-scatter.4
  1354.4 269.0 all-reduce.3
where the time goes:
time: 1650 us; the launch traced here: 1640 us
  waiting for transfers between devices  834 us (51%)
  blocking collectives  294 us (18%)
  local copies, waits for them, and re-layouts  239 us (14%)
  matrix products  153 us (9%)
  other arithmetic  86.7 us (5%)
  starting transfers between devices  19.9 us (1%)
    all_to_all x1, blocking collectives, local(): lax.all_to_all(slot_upstream, 'ep', split_axis=1, concat_axis=0, tiled=True)  219 us
    all_gather x1, waiting for transfers between devices, local(): lax.all_gather(upstream_recv, 'hs', axis=0, tiled=True)  175 us
    psum x1, waiting for transfers between devices, local(): lax.psum((attn_gain_grad, query_w_grad, key_w_grad, value_w_grad, out_w_g...  159 us
    reduce_scatter x1, waiting for transfers between devices, local(): lax.psum_scatter(input_partial(gate_pre_grad, up_pre_grad, w_gate, w_up)....  158 us
    reduce_scatter x1, waiting for transfers between devices, local(): lax.psum_scatter(expert_rows(gathered, w_gate, w_up, w_down).astype(jnp.b...  151 us
    unnamed x170, local copies, waits for them, and re-layouts  107 us
    all_to_all x1, waiting for transfers between devices, local(): lax.all_to_all(dispatched, 'ep', split_axis=1, concat_axis=0, tiled=True)  105 us
    all_to_all x1, waiting for transfers between devices, local(): lax.all_to_all(input_sum, 'ep', split_axis=0, concat_axis=1, tiled=True)  86.6 us
  transfers between devices with their start and end apart: 8, of which 6 were waited for; matrix products, arithmetic and copies ran while one was open for 17% of the time, Pallas kernels for 0%

commit v1 on v0

--- a/solution.py
+++ b/solution.py
@@ -333,17 +333,20 @@
     input_norm_grad, attn_gain_grad = rms_backward(inputs, inverse_one, attn_gain, normed_grad)
     input_grad = middle_grad + input_norm_grad
     shared = lax.psum(
-        (
-            attn_gain_grad,
-            query_w_grad,
-            key_w_grad,
-            value_w_grad,
-            out_w_grad,
-            moe_gain_grad,
-            router_w_grad,
-            counts_local,
+        lax.psum(
+            (
+                attn_gain_grad,
+                query_w_grad,
+                key_w_grad,
+                value_w_grad,
+                out_w_grad,
+                moe_gain_grad,
+                router_w_grad,
+                counts_local,
+            ),
+            "hs",
         ),
-        ("ep", "hs"),
+        "ep",
     )
     return (
         output,

time: 1650 us -> 1950 us (1.18)
  waiting for transfers between devices: 834 us -> 1160 us
  blocking collectives: 294 us -> 261 us
    psum x0 -> x1, waiting for transfers between devices: none -> 167 us  [local(): lax.psum(lax.psum((attn_gain_grad, query_w_grad, key_w_grad, value_w_grad...]
    psum x1, waiting for transfers between devices: 159 us -> 323 us  [local(): lax.psum((attn_gain_grad, query_w_grad, key_w_grad, value_w_grad, out_w_g...]
    psum x1, blocking collectives: 75 us -> 5.02 us  [local(): lax.psum((attn_gain_grad, query_w_grad, key_w_grad, value_w_grad, out_w_g...]
    psum x0 -> x1, blocking collectives: none -> 37.2 us  [local(): lax.psum(lax.psum((attn_gain_grad, query_w_grad, key_w_grad, value_w_grad...]
  transfers between devices with their start and end apart: 8 -> 9, of which waited for: 6 -> 7; matrix products, arithmetic and copies ran while one was open for 17% -> 14% of each run, Pallas kernels for 0% -> 0%
where the time goes in v1:
time: 1950 us; the launch traced here: 1940 us
  waiting for transfers between devices  1160 us (59%)
  blocking collectives  261 us (13%)
  local copies, waits for them, and re-layouts  239 us (12%)
  matrix products  153 us (8%)
  other arithmetic  86.3 us (4%)
  starting transfers between devices  20.2 us (1%)
    psum x1, waiting for transfers between devices, local(): lax.psum((attn_gain_grad, query_w_grad, key_w_grad, value_w_grad, out_w_g...  323 us
    all_to_all x1, blocking collectives, local(): lax.all_to_all(slot_upstream, 'ep', split_axis=1, concat_axis=0, tiled=True)  219 us
    all_gather x1, waiting for transfers between devices, local(): lax.all_gather(upstream_recv, 'hs', axis=0, tiled=True)  175 us
    psum x1, waiting for transfers between devices, local(): lax.psum(lax.psum((attn_gain_grad, query_w_grad, key_w_grad, value_w_grad...  167 us
    reduce_scatter x1, waiting for transfers between devices, local(): lax.psum_scatter(input_partial(gate_pre_grad, up_pre_grad, w_gate, w_up)....  158 us
    reduce_scatter x1, waiting for transfers between devices, local(): lax.psum_scatter(expert_rows(gathered, w_gate, w_up, w_down).astype(jnp.b...  151 us
    unnamed x170, local copies, waits for them, and re-layouts  107 us
    all_to_all x1, waiting for transfers between devices, local(): lax.all_to_all(dispatched, 'ep', split_axis=1, concat_axis=0, tiled=True)  105 us
  transfers between devices with their start and end apart: 9, of which 7 were waited for; matrix products, arithmetic and copies ran while one was open for 14% of the time, Pallas kernels for 0%

profile of v1, /device:TPU:0, one launch (start us, length us, event | category | flops | bytes accessed | tf_op | source)
XLA Modules:
  0.0 1940.4 jit_solution(6646654676125448095)
XLA Ops:
  12.1 4.5 reduce-window.19
  17.4 8.1 scatter_custom_fusion.1
  25.5 8.3 scatter_custom_fusion
  46.6 18.3 gather_fusion
  64.9 16.9 copy_select_fusion
  81.8 7.5 all-to-all-start
  93.2 23.0 %gather_fusion.2 = f32[4096]{0:T(1024)S(1)} fusion(f32[2048]{0:T(1024)S(1)} %mul.462, s32[4096]{0:T(1024)S(1)} %get-tuple-element.50), kind=kCustom, calls=%fused_computation.2 | custom fusion | bytes 49152 | tf_op jit(solution)/shard_map/gather | solution.py:230
  116.4 18.6 gather_fusion.3
  135.0 105.1 %all-to-all-done = bf16[256,16,1024]{2,0,1:T(8,128)(2,1)} async-done(((bf16[256,16,1024]{2,0,1:T(8,128)(2,1)}), bf16[256,16,1024]{2,0,1:T(8,128)(2,1)}, u32[]{:S(2)}, u32[]{:S(2)}) %all-to-all-start) | async-done | bytes 8388640 | tf_op jit(solution)/shard_map/all_to_all | solution.py:212
  240.4 15.4 fusion.14
  255.8 218.9 %all_to_all.66 = bf16[256,16,1024]{2,0,1:T(8,128)(2,1)} all-to-all(bf16[256,16,1024]{2,0,1:T(8,128)(2,1)S(1)} %fusion.14), channel_id=1, replica_groups=mesh['ep'=16,'hs'=2] {'ep'}, dimensions={1} | all-to-all | bytes 16777216 | tf_op jit(solution)/shard_map/all_to_all | solution.py:235
  475.8 15.3 fusion.18
  493.1 7.1 fusion.15
  500.2 174.6 %all-gather.5.cloned.1.call-done = bf16[8192,1,1024]{2,0,1:T(8,128)(2,1)} async-done(((bf16[4096,1,1024]{2,0,1:T(8,128)(2,1)}), bf16[8192,1,1024]{2,0,1:T(8,128)(2,1)}) %all-gather.5.cloned.1.call-update) | async-done | bytes 16777232 | tf_op jit(solution)/shard_map/all_gather | solution.py:238
  674.8 22.0 %fusion.28 = (bf16[8192,256]{1,0:T(8,128)(2,1)}, bf16[8192,1,256]{2,0,1:T(8,128)(2,1)}, bf16[8192,256]{1,0:T(8,128)(2,1)}) fusion(f32[8192,1,256]{2,0,1:T(8,128)} %fusion.15, f32[8192,1,256]{2,0,1:T(8,128)} %fusion.18, bf16[1,256,1024]{2,1,0:T(8,128)(2,1)S(1)} %copy-done.41, bf16[8192,1,1024]{2,0,1:T(8,128)(2,1)} %all-gather.5.cloned.1.call-done), kind=kOutput, calls=%fused_computation.40 | convolution fusion | flops 4326424576 | bytes 46661632 | tf_op jit(solution)/shard_map/red,efd->ref/dot_general | solution.py:92
  696.8 10.4 convert_bitcast_fusion
  707.5 18.4 fusion.33
  725.9 19.8 %fusion = bf16[8192,1,1024]{2,0,1:T(8,128)(2,1)} fusion(f32[8192,1024]{1,0:T(8,128)} %fusion.33, bf16[8192,256]{1,0:T(8,128)(2,1)S(1)} %copy-done.11, bf16[1,1024,256]{2,1,0:T(8,128)(2,1)} %param.27), kind=kOutput, calls=%fused_computation.8 | convolution fusion | flops 4311744512 | bytes 55050240 | tf_op jit(solution)/shard_map/ref,edf->red/dot_general | solution.py:111
  745.7 150.9 %reduce-scatter.3.cloned.1.call-done = bf16[4096,1,1024]{2,0,1:T(8,128)(2,1)} async-done(((bf16[8192,1,1024]{2,0,1:T(8,128)(2,1)}), bf16[4096,1,1024]{2,0,1:T(8,128)(2,1)}) %reduce-scatter.3.cloned.1.call-update) | async-done | bytes 8388624 | tf_op jit(solution)/shard_map/reduce_scatter | solution.py:214
  897.1 12.7 reduce.13
  909.8 14.7 reshape.555
  924.5 5.9 all-to-all-start.1
  930.4 157.6 %reduce-scatter.5.cloned.1.call-done = bf16[4096,1,1024]{2,0,1:T(8,128)(2,1)} async-done(((bf16[8192,1,1024]{2,0,1:T(8,128)(2,1)}), bf16[4096,1,1024]{2,0,1:T(8,128)(2,1)}) %reduce-scatter.5.cloned.1.call-update) | async-done | bytes 8388624 | tf_op jit(solution)/shard_map/reduce_scatter | solution.py:243
  1088.0 12.7 reduce.12
  1100.7 14.5 reshape.557
  1115.2 5.8 all-to-all-start.3
  1121.1 16.7 reshape.556
  1137.9 12.1 copy.162
  1150.0 11.3 copy.141
  1161.3 15.5 gather_fusion.1
  1176.9 6.1 fusion.25
  1185.1 86.6 %all-to-all-done.3 = bf16[16,2,131072]{2,1,0:T(2,128)(2,1)} async-done(((bf16[16,2,131072]{2,1,0:T(2,128)(2,1)}), bf16[16,2,131072]{2,1,0:T(2,128)(2,1)}, u32[]{:S(2)}, u32[]{:S(2)}) %all-to-all-start.3) | async-done | bytes 8388640 | tf_op jit(solution)/shard_map/all_to_all | solution.py:249
  1271.7 16.3 reshape.558
  1288.1 12.3 copy.163
  1300.3 11.3 copy.146
  1311.7 15.6 gather_fusion.4
  1327.3 5.6 convert_reduce_fusion
  1336.8 3.1 fusion.60
  1351.5 2.8 fusion.109
  1354.6 323.0 %all-reduce.9.cloned.1.call-done = (f32[1024,1024]{1,0:T(8,128)}, f32[1024,512]{1,0:T(8,128)}, f32[1024,512]{1,0:T(8,128)}, f32[1024,1024]{1,0:T(8,128)}, f32[1024,16]{0,1:T(8,128)}) async-done(((f32[1024,1024]{1,0:T(8,128)}, f32[1024,512]{1,0:T(8,128)}, f32[1024,512]{1,0:T(8,128)}, f32[1024,1024]{1,0:T(8,128)}, f32[1024,16]{0,1:T(8,128)}), (f32[1024,1024]{1,0:T(8,128)}, f32[1024,512]{1,0:T(8,128)}, ...) | async-done | bytes 12648464 | tf_op jit(solution)/shard_map/psum | solution.py:336
  1677.6 12.6 fusion.49
  1690.2 9.5 fusion.41
  1700.4 5.5 fusion.46
  1709.3 5.0 all-reduce.2
  1714.3 37.2 %all-reduce = (f32[1024]{0:T(1024)}, f32[1024]{0:T(1024)}, f32[16]{0:T(128)S(1)}) all-reduce(f32[1024]{0:T(1024)S(1)} %get-tuple-element.29, f32[1024]{0:T(1024)S(1)} %get-tuple-element.30, f32[16]{0:T(128)S(1)} %get-tuple-element.31), channel_id=1, replica_groups=mesh['ep'=16,'hs'=2] {'ep'}, use_global_device_ids=true, to_apply=%region_26.27 | all-reduce | flops 2064 | bytes 16512 | tf_op jit(solution)/shard_map/psum | solution.py:335
  1752.0 2.9 fusion.67
  1754.9 166.9 %all-reduce.7.cloned.1.call-done = (f32[1024,1024]{1,0:T(8,128)}, f32[1024,512]{1,0:T(8,128)}, f32[1024,512]{1,0:T(8,128)}, f32[1024,1024]{1,0:T(8,128)}, f32[1024,16]{0,1:T(8,128)}) async-done(((f32[1024,1024]{1,0:T(8,128)}, f32[1024,512]{1,0:T(8,128)}, f32[1024,512]{1,0:T(8,128)}, f32[1024,1024]{1,0:T(8,128)}, f32[1024,16]{0,1:T(8,128)}), (f32[1024,1024]{1,0:T(8,128)}, f32[1024,512]{1,0:T(8,128)}, ...) | async-done | bytes 12648464 | tf_op jit(solution)/shard_map/psum | solution.py:335
  1921.8 4.9 copy.184
  (259 shorter events, 54.8 us)
Async XLA Ops:
  7.2 37.5 %copy-start = (bf16[1024,1024]{1,0:T(8,128)(2,1)S(1)}, bf16[1024,1024]{1,0:T(8,128)(2,1)}, u32[]{:S(2)}) copy-start(bf16[1024,1024]{1,0:T(8,128)(2,1)} %param.23) | copy-start | bytes 6291460
  7.2 28.9 %copy-start.7 = (bf16[256,1024]{1,0:T(8,128)(2,1)S(1)}, bf16[256,1024]{1,0:T(8,128)(2,1)}, u32[]{:S(2)}) copy-start(bf16[256,1024]{1,0:T(8,128)(2,1)} %param.15) | copy-start | bytes 1572868
  7.2 28.9 %copy-start.48 = (f32[1024]{0:T(1024)S(1)}, f32[1024]{0:T(1024)}, u32[]{:S(2)}) copy-start(f32[1024]{0:T(1024)} %param.19) | copy-start | bytes 12292
  12.0 28.6 %copy-start.59 = (f32[256]{0:T(256)}, f32[256]{0:T(256)S(1)}, u32[]{:S(2)}) copy-start(f32[256]{0:T(256)S(1)} %add_rsqrt_fusion.1) | copy-start | bytes 3076
  17.4 16.4 copy-start.63
  36.1 7.2 copy-start.33
  45.5 19.4 %copy-start.72 = (f32[256]{0:T(256)}, f32[256]{0:T(256)S(1)}, u32[]{:S(2)}) copy-start(f32[256]{0:T(256)S(1)} %add_rsqrt_fusion) | copy-start | bytes 3076
  46.6 18.3 copy-start.3
  81.8 7.6 copy-start.74
  81.8 8.8 copy-start.50
  81.8 10.5 copy-start.52
  81.8 158.3 %all-to-all-start = ((bf16[256,16,1024]{2,0,1:T(8,128)(2,1)}), bf16[256,16,1024]{2,0,1:T(8,128)(2,1)}, u32[]{:S(2)}, u32[]{:S(2)}) async-start(bf16[256,16,1024]{2,0,1:T(8,128)(2,1)} %copy_select_fusion), calls=%async_computation | async-start | bytes 16777216 | tf_op jit(solution)/shard_map/all_to_all | solution.py:212
  89.4 385.4 %all-gather.3.cloned.1.call-start = ((), (), s32[]{:S(2)}) async-start(), calls=%async_computation.6 | async-start | bytes 25165824 | tf_op jit(solution)/shard_map/all_gather | solution.py:213
  90.6 25.8 %copy-start.1 = (f32[256,1024]{1,0:T(8,128)}, f32[256,1024]{1,0:T(8,128)S(1)}, u32[]{:S(2)}) copy-start(f32[256,1024]{1,0:T(8,128)S(1)} %convert_element_type.172) | copy-start | bytes 3145732
  93.1 23.2 %copy-start.26 = (f32[256,8]{1,0:T(8,128)}, f32[256,8]{1,0:T(8,128)S(1)}, u32[]{:S(2)}) copy-start(f32[256,8]{1,0:T(8,128)S(1)} %copy.134) | copy-start | bytes 24580
  240.1 434.7 %all-gather.5.cloned.1.call-start = ((), (), s32[]{:S(2)}) async-start(), calls=%async_computation.8 | async-start | bytes 25165824 | tf_op jit(solution)/shard_map/all_gather | solution.py:238
  474.7 16.3 copy-start.39
  474.8 421.8 %reduce-scatter.3.cloned.1.call-start = ((), (), s32[]{:S(2)}) async-start(), calls=%async_computation.7 | async-start | bytes 25165824 | tf_op jit(solution)/shard_map/reduce_scatter | solution.py:214
  475.8 17.3 copy-start.4
  493.1 181.8 %copy-start.41 = (bf16[1,256,1024]{2,1,0:T(8,128)(2,1)S(1)}, bf16[1,256,1024]{2,1,0:T(8,128)(2,1)}, u32[]{:S(2)}) copy-start(bf16[1,256,1024]{2,1,0:T(8,128)(2,1)} %param.28) | copy-start | bytes 1572868
  707.3 380.7 %reduce-scatter.5.cloned.1.call-start = ((), (), s32[]{:S(2)}) async-start(), calls=%async_computation.9 | async-start | bytes 25165824 | tf_op jit(solution)/shard_map/reduce_scatter | solution.py:243
  707.5 18.4 copy-start.11
  924.5 190.7 %all-to-all-start.1 = ((bf16[16,2,131072]{2,1,0:T(2,128)(2,1)}), bf16[16,2,131072]{2,1,0:T(2,128)(2,1)}, u32[]{:S(2)}, u32[]{:S(2)}) async-start(bf16[16,2,131072]{2,1,0:T(2,128)(2,1)} %reshape.555), calls=%async_computation.2 | async-start | bytes 16777216 | tf_op jit(solution)/shard_map/all_to_all | solution.py:220
  1115.2 5.9 copy-start.64
  1115.2 5.9 copy-start.55
  1115.2 5.9 copy-start.57
  1115.2 156.5 %all-to-all-start.3 = ((bf16[16,2,131072]{2,1,0:T(2,128)(2,1)}), bf16[16,2,131072]{2,1,0:T(2,128)(2,1)}, u32[]{:S(2)}, u32[]{:S(2)}) async-start(bf16[16,2,131072]{2,1,0:T(2,128)(2,1)} %reshape.557), calls=%async_computation.5 | async-start | bytes 16777216 | tf_op jit(solution)/shard_map/all_to_all | solution.py:249
  1121.0 556.5 %all-reduce.9.cloned.1.call-start = ((), (), s32[]{:S(2)}) async-start(), calls=%async_computation.11 | async-start | bytes 25296896 | tf_op jit(solution)/shard_map/psum | solution.py:336
  1161.3 15.5 copy-start.2
  1161.3 15.5 copy-start.27
  1176.8 6.2 copy-start.47
  1176.8 6.2 copy-start.66
  1176.8 6.2 copy-start.68
  1176.9 6.2 copy-start.70
  1176.9 6.2 copy-start.53
  1327.3 5.7 copy-start.13
  1327.3 5.7 copy-start.51
  1327.3 6.3 copy-start.18
  1327.3 6.3 copy-start.23
  1354.3 567.5 %all-reduce.7.cloned.1.call-start = ((), (), s32[]{:S(2)}) async-start(), calls=%async_computation.10 | async-start | bytes 25296896 | tf_op jit(solution)/shard_map/psum | solution.py:335
  1677.6 12.6 copy-start.9
  1677.6 22.1 %slice-start = ((s8[16777216]{0:T(1024)(128)(4,1)}), s8[4194304]{0:T(1024)(128)(4,1)S(1)}, s32[]{:S(2)}) async-start(s8[16777216]{0:T(1024)(128)(4,1)} %bitcast.245), calls=%async_computation.12 | async-start | bytes 8388608
  1677.6 22.1 %slice-start.1 = ((s8[16777216]{0:T(1024)(128)(4,1)}), s8[4194304]{0:T(1024)(128)(4,1)S(1)}, s32[]{:S(2)}) async-start(s8[16777216]{0:T(1024)(128)(4,1)} %bitcast.245), calls=%async_computation.13 | async-start | bytes 8388608
  1690.2 9.5 slice-start.2
  1690.2 9.5 slice-start.3
  1690.2 10.2 copy-start.10
  1700.4 6.3 copy-start.20
  1921.8 6.3 copy-start.21
  (40 other events, 95.9 us)
Sparse Core Ops, SparseCore 0:
  240.2 230.6 all-gather.2
  474.9 199.8 all-gather.4
  707.4 189.1 reduce-scatter.2
  898.8 189.1 reduce-scatter.4
  1354.4 323.0 all-reduce.8
  1682.5 239.3 all-reduce.6
